TPU v7x, 256 devices: a whole 4x4x8 slice. The times are simulated.
256 devices in a mesh: space: 16 (over z, x_hi), mrow: 4 (over y), mcol: 4 (over x_lo, core).
Axes of the slice: x: 4 (x_hi: 2, x_lo: 2; x = x_hi * 2 + x_lo), y: 4, z: 8, core: 2. Of those that a mesh axis runs over, the one named last changes fastest.
Arguments:
- deviation: bfloat16 [512, 48, 8192], P('space', None, ('mcol', 'mrow'))
- courant: float32 [2, 8192], P(None, ('mcol', 'mrow')), may hold values from -0.95 to 0.95
- collide: bfloat16 [8192, 8192], P('mrow', ('mcol', 'space'))
- hole_cells: int32 [6144], P('space'), may hold values from -1 to 1535, as said below
- hole_wall: int32 [6144], P('space'), may hold values from 0 to 3
- specular: int32 [4, 8192], replicated, may hold values from 0 to 8191, as said below
- specularity: float32 [4], replicated, may hold values from 0.2 to 0.8
Outputs:
- updated: bfloat16 [512, 48, 8192], P('space', None, ('mrow', 'mcol'))
Inputs may be any that keep to these rules, and one draw needn't show every extreme that they name: `hole_cells`: within one tile the used slots come first and name distinct cells; every tile has at least 96 used slots, some tile has all 384 slots used and some tile has an empty slot. Each row specular[w] is a permutation of the modes; for an outgoing mode i of aligned block e = i // 512, its incoming mode j lies, within j's own aligned block of 512 modes, in the sub-block of 32 modes numbered e, that is (j % 512) // 32 == e.
All inputs are finite; a program needn't handle non-finite values.
Results may differ from a plain program's by a relative error of at most 0.005.
Values may be sent and summed in bfloat16 or wider, within the bound.
A program may use at most 128 MiB of HBM per device.

v0:
```python
import jax
import jax.numpy as jnp
from jax import lax
from jax.sharding import PartitionSpec as P


def extended(x, sides, width):
    for axis, dim in sides:
        size, length = (lax.axis_size(axis), x.shape[dim])
        up = [(i, (i + 1) % size) for i in range(size - 1)]
        down = [(j, i) for i, j in up]
        last = lax.slice_in_dim(x, length - width, length, axis=dim)
        first = lax.slice_in_dim(x, 0, width, axis=dim)
        before = lax.ppermute(last, axis, up)
        after = lax.ppermute(first, axis, down)
        x = jnp.concatenate([before, x, after], axis=dim)
    return x


def upwind(padded, courant):
    field = padded.astype(jnp.float32)
    reach_x = jnp.abs(courant[0])
    reach_y = jnp.abs(courant[1])
    center = field[1:-1]
    upwind_x = jnp.where(courant[0] > 0, field[:-2], field[2:])
    upwind_y = jnp.where(courant[1] > 0, jnp.roll(center, 1, axis=1), jnp.roll(center, -1, axis=1))
    upwind_xy = jnp.where(
        courant[1] > 0, jnp.roll(upwind_x, 1, axis=1), jnp.roll(upwind_x, -1, axis=1)
    )
    result = (1.0 - reach_x) * (1.0 - reach_y) * center + reach_x * (1.0 - reach_y) * upwind_x
    result = result + (1.0 - reach_x) * reach_y * upwind_y + reach_x * reach_y * upwind_xy
    return result.astype(jnp.bfloat16)


def mirror_values(source_rows, wall_tables, one_hot):
    flipped = source_rows.T
    picked = flipped[wall_tables].astype(jnp.float32)
    weights = one_hot.T.astype(jnp.float32)
    chosen = jnp.sum(weights[:, None, :] * picked, axis=0)
    return chosen.T


def reemit(full_rows, wall_tables, one_hot, share):
    mirrored = mirror_values(full_rows, wall_tables, one_hot)
    diffuse = jnp.sum(full_rows.astype(jnp.float32), axis=1) / full_rows.shape[1]
    return (share[:, None] * mirrored + (1.0 - share)[:, None] * diffuse[:, None]).astype(
        jnp.bfloat16
    )


def on_device(deviation, courant, collide, hole_cells, hole_wall, specular, specularity):
    padded = extended(deviation, (("space", 0),), 1)
    read = upwind(padded, courant)
    width_x, width_y, block_len = read.shape
    cell_count = width_x * width_y
    row_groups = lax.axis_size("mrow")
    col_groups = lax.axis_size("mcol")
    is_live = hole_cells >= 0
    safe_ids = jnp.where(is_live, hole_cells, 0)
    target_ids = jnp.where(is_live, hole_cells, cell_count)
    wall_count = specular.shape[0]
    one_hot = hole_wall[:, None] == jnp.arange(wall_count, dtype=jnp.int32)[None, :]
    share = jnp.dot(one_hot.astype(jnp.float32), specularity, precision=lax.Precision.HIGHEST)
    flat_cells = read.reshape(cell_count, block_len)
    start = (lax.axis_index("mcol") * row_groups + lax.axis_index("mrow")) * block_len
    own_table = lax.dynamic_slice_in_dim(specular, start, block_len, 1)
    block_ids = own_table // block_len
    positions = (
        block_ids % row_groups * col_groups + block_ids // row_groups
    ) * block_len + own_table % block_len
    full_rows = lax.all_gather(flat_cells[safe_ids], ("mrow", "mcol"), axis=1, tiled=True)
    emitted = reemit(full_rows, positions, one_hot, share)
    flat_cells = flat_cells.at[target_ids].set(emitted, mode="drop")
    columns = lax.all_gather(
        flat_cells.reshape(width_x, width_y, block_len), "mrow", axis=2, tiled=True
    )
    column_flat = columns.reshape(cell_count, columns.shape[2])
    partial_sums = lax.dot_general(
        column_flat,
        lax.all_gather(collide, "space", axis=1, tiled=True),
        (((1,), (1,)), ((), ())),
        preferred_element_type=jnp.float32,
    )
    summed = lax.psum_scatter(partial_sums, "mcol", scatter_dimension=1, tiled=True)
    return summed.astype(jnp.bfloat16).reshape(width_x, width_y, summed.shape[1])


def solution(mesh):
    in_specs = (
        P("space", None, ("mcol", "mrow")),
        P(None, ("mcol", "mrow")),
        P("mrow", ("mcol", "space")),
        P("space"),
        P("space"),
        P(),
        P(),
    )
    out_specs = P("space", None, ("mrow", "mcol"))
    return jax.shard_map(
        on_device, mesh=mesh, in_specs=in_specs, out_specs=out_specs, check_vma=False
    )
```

profile of v0, /device:TPU:1, one launch (start us, length us, event | category | flops | bytes accessed | tf_op | source)
XLA Modules:
  0.0 448.5 jit_solution(13947178258278800401)
XLA Ops:
  6.5 0.8 fusion.22
  7.4 5.5 %collective-permute-start = (bf16[1,48,512]{2,1,0:T(8,128)(2,1)S(1)}, bf16[1,48,512]{2,1,0:T(8,128)(2,1)S(1)}, u32[]{:S(2)}, u32[]{:S(2)}) collective-permute-start(bf16[1,48,512]{2,1,0:T(8,128)(2,1)S(1)} %get-tuple-element.15), channel_id=1, source_target_pairs={{0,16},{16,32},{32,48},{48,64},{64,80},{80,96},{96,112},{112,128},... | collective-permute-start | bytes 147464 | tf_op jit(solution)/shard_map/ppermute | solution.py:14
  12.8 1.3 collective-permute-start.1
  14.1 0.8 compare_reduce_fusion
  14.9 0.8 slice_abs_fusion
  16.4 2.8 collective-permute-done.1
  19.2 1.7 maximum_convert_fusion
  21.5 4.9 %fusion.19 = (f32[32,47,512]{2,1,0:T(8,128)}, f32[32,47,512]{2,1,0:T(8,128)}, f32[32,47,512]{2,1,0:T(8,128)}, f32[32,47,512]{2,1,0:T(8,128)}) fusion(f32[34,48,512]{2,1,0:T(8,128)S(1)} %maximum_convert_fusion, f32[32,48,512]{2,1,0:T(8,128)S(1)} %slice_select_fusion), kind=kLoop, calls=%fused_computation.62 | loop fusion | bytes 24641536 | tf_op jit(solution)/shard_map/jit(_roll_static)/slice | solution.py:26
  26.5 1.1 maximum_convert_fusion.1
  27.6 6.2 %fusion.3 = bf16[32,48,512]{2,1,0:T(8,128)(2,1)S(1)} fusion(f32[34,48,512]{2,1,0:T(8,128)S(1)} %maximum_convert_fusion, f32[32,47,512]{2,1,0:T(8,128)} %get-tuple-element.8, f32[32,1,512]{2,1,0:T(1,128)S(1)} %get-tuple-element.14, f32[32,1,512]{2,1,0:T(1,128)S(1)} %get-tuple-element.13, f32[32,47,512]{2,1,0:T(8,128)} %get-tuple-element.7, ...), kind=kLoop, calls=%fused_computation.9 | loop fusion | flops 11796480 | bytes 23602176 | tf_op jit(solution)/shard_map/convert_element_type | solution.py:32
  33.9 2.6 gather_fusion
  36.5 0.7 all-gather.7.cloned.1.call-update
  37.3 0.7 fusion.16
  38.4 48.1 %all-gather.9.cloned.1.call-done = bf16[384,8192]{1,0:T(8,128)(2,1)} async-done(((bf16[384,512]{1,0:T(8,128)(2,1)}), bf16[384,8192]{1,0:T(8,128)(2,1)}) %all-gather.9.cloned.1.call-update) | async-done | bytes 6291472 | tf_op jit(solution)/shard_map/all_gather | solution.py:71
  86.5 8.7 %copy.9 = bf16[8192,384]{1,0:T(8,128)(2,1)} copy(bf16[8192,384]{0,1:T(8,128)(2,1)} %bitcast.22) | data formatting | bytes 12582912 | tf_op jit(solution)/shard_map/transpose | solution.py:36
  95.1 10.8 %gather_fusion.1 = bf16[2048,384]{1,0:T(8,128)(2,1)S(1)} fusion(bf16[8192,384]{1,0:T(8,128)(2,1)} %copy.9, s32[2048]{0:T(1024)S(1)} %broadcast_clamp_fusion), kind=kCustom, calls=%fused_computation.1 | custom fusion | bytes 3153920 | tf_op jit(solution)/shard_map/gather | solution.py:37
  106.3 3.7 convert_reduce_fusion
  110.3 2.8 scatter_fusion
  113.1 1.1 copy-done.2
  114.5 118.4 %all-gather.7.cloned.1.call-done = bf16[2048,2048]{1,0:T(8,128)(2,1)} async-done(((bf16[2048,128]{1,0:T(8,128)(2,1)}), bf16[2048,2048]{1,0:T(8,128)(2,1)}) %all-gather.7.cloned.1.call-update) | async-done | bytes 8388624 | tf_op jit(solution)/shard_map/all_gather | solution.py:80
  232.9 69.9 %all-gather.5.cloned.1.call-done = bf16[32,48,2048]{2,1,0:T(8,128)(2,1)} async-done(((bf16[32,48,512]{2,1,0:T(8,128)(2,1)}), bf16[32,48,2048]{2,1,0:T(8,128)(2,1)}) %all-gather.5.cloned.1.call-update) | async-done | bytes 6291472 | tf_op jit(solution)/shard_map/all_gather | solution.py:74
  302.9 19.0 %fusion.23 = f32[1536,2048]{1,0:T(8,128)} fusion(bf16[1536,2048]{1,0:T(8,128)(2,1)} %bitcast.27, bf16[2048,2048]{1,0:T(8,128)(2,1)} %all-gather.7.cloned.1.call-done), kind=kOutput, calls=%fused_computation.66 | convolution fusion | flops 12884901888 | bytes 27262976 | tf_op jit(solution)/shard_map/dot_general | solution.py:78
  322.0 116.8 %reduce-scatter.2.cloned.1.call-done = f32[1536,512]{1,0:T(8,128)} async-done(((f32[1536,2048]{1,0:T(8,128)}), f32[1536,512]{1,0:T(8,128)}) %reduce-scatter.2.cloned.1.call-update) | async-done | bytes 3145744 | tf_op jit(solution)/shard_map/reduce_scatter | solution.py:84
  438.7 3.2 convert_element_type.36
  (28 shorter events, 2.7 us)
Async XLA Ops:
  6.5 31.5 %copy-start = (f32[4]{0:T(128)S(1)}, f32[4]{0:T(128)}, u32[]{:S(2)}) copy-start(f32[4]{0:T(128)} %param.13) | copy-start | bytes 52
  6.5 79.9 %all-gather.9.cloned.1.call-start = ((), (), s32[]{:S(2)}) async-start(), calls=%async_computation.4 | async-start | bytes 6684672 | tf_op jit(solution)/shard_map/all_gather | solution.py:71
  7.4 9.0 %collective-permute-start = (bf16[1,48,512]{2,1,0:T(8,128)(2,1)S(1)}, bf16[1,48,512]{2,1,0:T(8,128)(2,1)S(1)}, u32[]{:S(2)}, u32[]{:S(2)}) collective-permute-start(bf16[1,48,512]{2,1,0:T(8,128)(2,1)S(1)} %get-tuple-element.15), channel_id=1, source_target_pairs={{0,16},{16,32},{32,48},{48,64},{64,80},{80,96},{96,112},{112,128},... | collective-permute-start | bytes 147464 | tf_op jit(solution)/shard_map/ppermute | solution.py:14
  12.8 6.3 %collective-permute-start.1 = (bf16[1,48,512]{2,1,0:T(8,128)(2,1)S(1)}, bf16[1,48,512]{2,1,0:T(8,128)(2,1)S(1)}, u32[]{:S(2)}, u32[]{:S(2)}) collective-permute-start(bf16[1,48,512]{2,1,0:T(8,128)(2,1)S(1)} %get-tuple-element.16), channel_id=1, source_target_pairs={{16,0},{32,16},{48,32},{64,48},{80,64},{96,80},{112,96},{128,112},... | collective-permute-start | bytes 147464 | tf_op jit(solution)/shard_map/ppermute | solution.py:15
  33.8 4.2 copy-start.3
  36.5 196.5 %all-gather.7.cloned.1.call-start = ((), (), s32[]{:S(2)}) async-start(), calls=%async_computation.2 | async-start | bytes 8912896 | tf_op jit(solution)/shard_map/all_gather | solution.py:80
  37.2 265.7 %all-gather.5.cloned.1.call-start = ((), (), s32[]{:S(2)}) async-start(), calls=%async_computation.1 | async-start | bytes 7864320 | tf_op jit(solution)/shard_map/all_gather | solution.py:74
  113.1 1.1 copy-start.2
  114.3 324.4 %reduce-scatter.2.cloned.1.call-start = ((), (), s32[]{:S(2)}) async-start(), calls=%async_computation.3 | async-start | bytes 15728640 | tf_op jit(solution)/shard_map/reduce_scatter | solution.py:84
  321.9 120.0 %copy-start.1 = (f32[4]{0:T(128)S(1)}, f32[4]{0:T(128)}, u32[]{:S(2)}) copy-start(f32[4]{0:T(128)} %param.13) | copy-start | bytes 52
Sparse Core Ops, SparseCore 0:
  36.6 49.8 all-gather.8
  88.9 143.9 all-gather.6
  234.8 68.0 all-gather.4
  322.1 116.6 reduce-scatter.1
where the time goes:
time: 449 us; the launch traced here: 448 us
  waiting for transfers between devices  357 us (80%)
  local copies, waits for them, and re-layouts  32.1 us (7%)
  other arithmetic  20 us (4%)
  matrix products  19.3 us (4%)
  between operations  13.3 us (3%)
  starting transfers between devices  7.05 us (2%)
    all_gather x1, waiting for transfers between devices, on_device(): lax.all_gather(collide, 'space', axis=1, tiled=True)  118 us
    reduce_scatter x1, waiting for transfers between devices, on_device(): lax.psum_scatter(partial_sums, 'mcol', scatter_dimension=1, tiled=True)  117 us
    all_gather x1, waiting for transfers between devices, on_device(): lax.all_gather(flat_cells.reshape(width_x, width_y, block_len), 'mrow', a...  69.9 us
    all_gather x1, waiting for transfers between devices, on_device(): lax.all_gather(flat_cells[safe_ids], ('mrow', 'mcol'), axis=1, tiled=True)  48.1 us
    dot_general x1, matrix products, on_device(): lax.dot_general(column_flat, lax.all_gather(collide, 'space', axis=1, til...  19 us
    gather x1, local copies, waits for them, and re-layouts, mirror_values(): picked = flipped[wall_tables].astype(jnp.float32)  10.8 us
  transfers between devices with their start and end apart: 6, of which 5 were waited for; matrix products, arithmetic and copies ran while one was open for 7% of the time, Pallas kernels for 0%

commit v1 on v0

v1 whole, which is shorter than its diff:
```python
import functools

import jax
import jax.numpy as jnp
from jax import lax
from jax.experimental import pallas as pl
from jax.experimental.pallas import tpu as pltpu
from jax.sharding import PartitionSpec as P

MESH = pl.DeviceIdType.MESH
F32 = jnp.float32
BF16 = jnp.bfloat16
CHUNKS = 4


def column_of(row, slots):
    return jnp.broadcast_to(row, (128, slots)).T


def widen(tile, count):
    return jnp.concatenate([tile] * count, axis=1)


def body(
    sizes,
    dev_ref,
    cour_ref,
    coll_ref,
    cells_ref,
    wall_ref,
    spec_ref,
    share_ref,
    out_ref,
    cols,
    mats,
    read_buf,
    halo,
    msg_out,
    msg_in,
    pair_out,
    pair_in,
    chip_out,
    chip_in,
    z_send,
    z_recv,
    x_send,
    x_recv,
    halo_send,
    halo_recv,
    msg_send,
    msg_recv,
    y_send,
    y_recv,
    pair_send,
    pair_recv,
    chip_send,
    chip_recv,
    own_sem,
):
    n_space, n_row, n_col = sizes
    depth = n_space // 2
    width_x, width_y, block = dev_ref.shape
    cells = width_x * width_y
    slots = cells_ref.shape[1]
    walls, modes = spec_ref.shape
    groups = n_row * n_col
    sub = block // groups
    chunk = cells // CHUNKS
    far = depth // 2
    half = block // 2

    s = lax.axis_index("space")
    y = lax.axis_index("mrow")
    q = lax.axis_index("mcol")
    z, h = s // 2, s % 2
    l, c = q // 2, q % 2
    mate_s = z * 2 + (1 - h)
    z_next = (s + 2) % n_space
    z_prev = (s + n_space - 2) % n_space
    other_s = (s + 2 * h - 1 + n_space) % n_space
    s_next = (s + 1) % n_space
    s_prev = (s + n_space - 1) % n_space
    y_next = (y + 1) % n_row
    y_prev = (y + n_row - 1) % n_row
    core_q = l * 2 + (1 - c)
    chip_q = (1 - l) * 2 + c
    blocks = (
        (1 - l) * 2 + (1 - c),
        (1 - l) * 2 + c,
        l * 2 + (1 - c),
        l * 2 + c,
    )
    mine = q * n_row + y

    peers = []
    for dq in range(n_col):
        for dy in range(n_row):
            if dq or dy:
                peers.append(((y + dy) % n_row, (q + dq) % n_col))

    barrier = pltpu.get_barrier_semaphore()
    for target in (z_next, z_prev, mate_s, other_s):
        pl.semaphore_signal(barrier, inc=1, device_id=(target, y, q), device_id_type=MESH)
    for ty, tq in peers:
        pl.semaphore_signal(barrier, inc=1, device_id=(s, ty, tq), device_id_type=MESH)
    pl.semaphore_wait(barrier, 4 + len(peers))

    started = []

    def remote(src, dst, send, recv, target):
        return pltpu.make_async_remote_copy(
            src_ref=src,
            dst_ref=dst,
            send_sem=send,
            recv_sem=recv,
            device_id=target,
            device_id_type=MESH,
        )

    def go(copy):
        copy.start()
        started.append(copy)

    def rows_of(turn, offset=0, size=None):
        size = block if size is None else size
        return pl.ds(pl.multiple_of(blocks[turn] * block + offset, size), size)

    def z_copy(way, group, hop, piece):
        turn = group * 2 + piece % 2
        if way == 0:
            source = (z + depth - (hop - 1)) % depth
            target = z_next
        else:
            source = (z + hop - 1) % depth
            target = z_prev
        slot = source * 2 + (h if piece < 2 else 1 - h)
        if hop == far:
            rows = rows_of(turn, way * half, half)
        else:
            rows = rows_of(turn)
        index = ((way * 2 + group) * far + hop - 1) * 4 + piece
        dst = mats.at[slot, rows]
        src = coll_ref.at[rows] if hop == 1 and piece < 2 else dst
        return remote(src, dst, z_send.at[index], z_recv.at[index], (target, y, q))

    def z_start(group, hop, pieces):
        for piece in pieces:
            for way in range(2):
                go(z_copy(way, group, hop, piece))

    def z_serve(group, hop, pieces):
        for piece in pieces:
            for way in range(2):
                z_copy(way, group, hop, piece).wait_recv()
                if hop < far:
                    go(z_copy(way, group, hop + 1, piece))

    def x_copy(turn):
        rows = rows_of(turn)
        return remote(
            coll_ref.at[rows],
            mats.at[s, rows],
            x_send.at[turn],
            x_recv.at[turn],
            (mate_s, y, q),
        )

    def y_copy(way, stage, part):
        target = y_next if way == 0 else y_prev
        if stage == 0:
            owner = y
            rows = pl.ds(part * chunk, chunk)
        else:
            owner = y_prev if way == 0 else y_next
            rows = pl.ds(part * chunk + way * (chunk // 2), chunk // 2)
        index = (way * 2 + stage) * CHUNKS + part
        ref = cols.at[owner, rows]
        return remote(ref, ref, y_send.at[index], y_recv.at[index], (s, target, q))

    def y_start(part):
        for way in range(2):
            go(y_copy(way, 0, part))

    def y_forward(part):
        for way in range(2):
            y_copy(way, 0, part).wait_recv()
            go(y_copy(way, 1, part))

    def y_finish(part):
        for way in range(2):
            y_copy(way, 1, part).wait_recv()

    def pair_copy(stage, part):
        rows = pl.ds(part * chunk, chunk)
        index = stage * CHUNKS + part
        return remote(
            pair_out.at[stage, rows],
            pair_in.at[stage, rows],
            pair_send.at[index],
            pair_recv.at[index],
            (s, y, core_q),
        )

    def chip_copy(part):
        rows = pl.ds(part * chunk, chunk)
        return remote(
            chip_out.at[rows],
            chip_in.at[rows],
            chip_send.at[part],
            chip_recv.at[part],
            (s, y, chip_q),
        )

    def product(turn, part):
        rows = pl.ds(part * chunk, chunk)
        total = None
        per = block // mats.shape[2]
        for owner in range(n_row):
            right = jnp.concatenate(
                [mats[owner * per + step, rows_of(turn), :] for step in range(per)], axis=1
            )
            term = lax.dot_general(
                cols[owner, rows, :],
                right,
                (((1,), (1,)), ((), ())),
                preferred_element_type=F32,
            )
            total = term if total is None else total + term
        return total

    halo_up = remote(
        dev_ref.at[width_x - 1], halo.at[0], halo_send.at[0], halo_recv.at[0], (s_next, y, q)
    )
    halo_down = remote(dev_ref.at[0], halo.at[1], halo_send.at[1], halo_recv.at[1], (s_prev, y, q))
    go(halo_up)
    go(halo_down)
    x_copies = [x_copy(turn) for turn in range(4)]
    go(x_copies[0])
    go(x_copies[1])
    z_start(0, 1, (0, 1))
    own_copy = pltpu.make_async_copy(coll_ref, mats.at[s], own_sem)
    own_copy.start()

    reach_x = jnp.abs(cour_ref[0:1, :])
    reach_y = jnp.abs(cour_ref[1:2, :])
    forward_x = cour_ref[0:1, :] > 0
    forward_y = cour_ref[1:2, :] > 0

    def stream(center, before, after):
        mixed = (1.0 - reach_x) * center + reach_x * jnp.where(forward_x, before, after)
        shifted = jnp.where(
            forward_y, pltpu.roll(mixed, 1, 0), pltpu.roll(mixed, width_y - 1, 0)
        )
        return ((1.0 - reach_y) * mixed + reach_y * shifted).astype(BF16)

    def layer(index):
        return dev_ref[index].astype(F32)

    @pl.loop(1, width_x - 1)
    def _(x):
        rows = pl.ds(pl.multiple_of(x * width_y, width_y), width_y)
        read_buf[rows, :] = stream(layer(x), layer(x - 1), layer(x + 1))

    halo_up.wait_recv()
    halo_down.wait_recv()
    low = jnp.where(s == 0, 0.0, halo[0].astype(F32))
    high = jnp.where(s == n_space - 1, 0.0, halo[1].astype(F32))
    read_buf[pl.ds(0, width_y), :] = stream(layer(0), low, layer(1))
    read_buf[pl.ds(cells - width_y, width_y), :] = stream(
        layer(width_x - 1), layer(width_x - 2), high
    )

    x_copies[0].wait_recv()
    x_copies[1].wait_recv()
    z_start(0, 1, (2, 3))

    cells_row = cells_ref[...].astype(F32)
    cells_col = column_of(cells_row, slots)
    lane = lax.broadcasted_iota(jnp.int32, (slots, 128), 1).astype(F32)
    pick = jnp.concatenate(
        [
            jnp.where(cells_col == lane + float(base), 1.0, 0.0).astype(BF16)
            for base in range(0, cells, 128)
        ],
        axis=1,
    )
    rim = jnp.dot(pick, read_buf[...], preferred_element_type=F32).T
    partial = jnp.sum(rim, axis=0, keepdims=True)
    first = partial.astype(BF16).astype(F32)
    second = (partial - first).astype(BF16).astype(F32)
    third = partial - first - second
    line = lax.broadcasted_iota(jnp.int32, (16, slots), 0)
    stats = jnp.where(
        line == 0, first, jnp.where(line == 1, second, jnp.where(line == 2, third, 0.0))
    ).astype(BF16)
    for e in range(groups):
        msg_out[e, 0:sub, :] = rim[e * sub : (e + 1) * sub].astype(BF16)
        msg_out[e, sub : sub + 16, :] = stats
    msg_copies = []
    for index, (ty, tq) in enumerate(peers):
        copy = remote(
            msg_out.at[tq * n_row + ty],
            msg_in.at[mine],
            msg_send.at[index],
            msg_recv.at[index],
            (s, ty, tq),
        )
        go(copy)
        msg_copies.append(copy)
    msg_in[mine] = msg_out[mine]
    go(x_copies[2])
    go(x_copies[3])

    z_serve(0, 1, (0, 1, 2))

    wall_col = column_of(wall_ref[...].astype(F32), slots)
    table = spec_ref[:, pl.ds(pl.multiple_of(mine * block, block), block)]
    place = (table // block) * sub + table % sub
    share = jnp.zeros((slots, 128), F32)
    for w in range(walls):
        share = jnp.where(wall_col == float(w), share_ref[w], share)

    for copy in msg_copies:
        copy.wait_recv()
    received = msg_in[...].astype(F32)
    inner = received[:, 0:sub, :].reshape(groups * sub, slots).T
    diffuse = jnp.sum(jnp.sum(received[:, sub : sub + 16, :], axis=0), axis=0, keepdims=True)
    diffuse = widen(column_of(diffuse / modes, slots), block // 128)
    spot = lax.broadcasted_iota(jnp.int32, (groups * sub, block), 0)
    mirrored = None
    for w in range(walls):
        chosen = jnp.where(widen(wall_col == float(w), block // 128), inner, 0.0).astype(BF16)
        route = jnp.where(spot == place[w : w + 1, :], 1.0, 0.0).astype(BF16)
        term = jnp.dot(chosen, route, preferred_element_type=F32)
        mirrored = term if mirrored is None else mirrored + term
    share = widen(share, block // 128)
    emitted = (share * mirrored + (1.0 - share) * diffuse).astype(BF16)
    emitted = jnp.concatenate([emitted, jnp.ones((slots, 128), BF16)], axis=1)

    spread = jnp.broadcast_to(cells_row, (chunk, slots))
    cell_of = lax.broadcasted_iota(jnp.int32, (chunk, slots), 0).astype(F32)

    def patch(part):
        rows = pl.ds(part * chunk, chunk)
        place_at = jnp.where(spread == cell_of + float(part * chunk), 1.0, 0.0).astype(BF16)
        placed = jnp.dot(place_at, emitted, preferred_element_type=F32)
        hole = widen(placed[:, block:], block // 128) > 0.5
        cols[y, rows, :] = jnp.where(
            hole, placed[:, :block], read_buf[rows, :].astype(F32)
        ).astype(BF16)

    patch(0)
    y_start(0)
    patch(1)
    y_start(1)
    patch(2)
    patch(3)

    z_serve(0, 1, (3,))
    z_serve(0, 2, (0, 1, 2, 3))
    y_forward(0)
    y_start(2)
    z_serve(0, 3, (0, 1))
    y_forward(1)
    y_start(3)
    z_serve(0, 3, (2, 3))
    x_copies[2].wait_recv()
    x_copies[3].wait_recv()
    z_start(1, 1, (0, 1, 2, 3))
    z_serve(0, 4, (0, 1, 2, 3))
    own_copy.wait()

    def pass_on(part):
        rows = pl.ds(part * chunk, chunk)
        pair_out[0, rows, :] = product(0, part)
        go(pair_copy(0, part))
        total = product(1, part)
        pair_copy(0, part).wait_recv()
        chip_out[rows, :] = (total + pair_in[0, rows, :]).astype(BF16)
        go(chip_copy(part))

    y_finish(0)
    pass_on(0)
    y_forward(2)
    z_serve(1, 1, (0, 1))
    y_finish(1)
    pass_on(1)
    z_serve(1, 1, (2, 3))
    y_forward(3)
    z_serve(1, 2, (0, 1, 2, 3))
    y_finish(2)
    pass_on(2)
    y_finish(3)
    pass_on(3)
    z_serve(1, 3, (0, 1, 2, 3))
    z_serve(1, 4, (0, 2))
    for part in range(CHUNKS):
        rows = pl.ds(part * chunk, chunk)
        pair_out[1, rows, :] = product(2, part)
        go(pair_copy(1, part))
    z_serve(1, 4, (1, 3))
    for part in range(CHUNKS):
        rows = pl.ds(part * chunk, chunk)
        total = product(3, part)
        pair_copy(1, part).wait_recv()
        chip_copy(part).wait_recv()
        out_ref[rows, :] = (
            total + pair_in[1, rows, :] + chip_in[rows, :].astype(F32)
        ).astype(BF16)
    for copy in started:
        copy.wait_send()


def on_device(sizes, deviation, courant, collide, hole_cells, hole_wall, specular, specularity):
    width_x, width_y, block = deviation.shape
    cells = width_x * width_y
    n_space, n_row, n_col = sizes
    groups = n_row * n_col
    slots = hole_cells.shape[0]
    rows, piece = collide.shape
    vmem = pl.BlockSpec(memory_space=pltpu.VMEM)
    smem = pl.BlockSpec(memory_space=pltpu.SMEM)
    dma = pltpu.SemaphoreType.DMA
    hops = 2 * 2 * (n_space // 4) * 4
    ways = 2 * 2 * CHUNKS
    sub = block // groups
    result = pl.pallas_call(
        functools.partial(body, sizes),
        out_shape=jax.ShapeDtypeStruct((cells, block), BF16),
        in_specs=[vmem] * 6 + [smem],
        out_specs=vmem,
        scratch_shapes=[
            pltpu.VMEM((n_row, cells, block), BF16),
            pltpu.VMEM((n_space, rows, piece), BF16),
            pltpu.VMEM((cells, block), BF16),
            pltpu.VMEM((2, width_y, block), BF16),
            pltpu.VMEM((groups, sub + 16, slots), BF16),
            pltpu.VMEM((groups, sub + 16, slots), BF16),
            pltpu.VMEM((2, cells, block), F32),
            pltpu.VMEM((2, cells, block), F32),
            pltpu.VMEM((cells, block), BF16),
            pltpu.VMEM((cells, block), BF16),
            dma((hops,)),
            dma((hops,)),
            dma((4,)),
            dma((4,)),
            dma((2,)),
            dma((2,)),
            dma((groups - 1,)),
            dma((groups - 1,)),
            dma((ways,)),
            dma((ways,)),
            dma((2 * CHUNKS,)),
            dma((2 * CHUNKS,)),
            dma((CHUNKS,)),
            dma((CHUNKS,)),
            dma(()),
        ],
        compiler_params=pltpu.CompilerParams(
            collective_id=0, has_side_effects=True, vmem_limit_bytes=60 * 2**20
        ),
        name="iterate",
    )(
        deviation,
        courant,
        collide,
        hole_cells.reshape(1, slots),
        hole_wall.reshape(1, slots),
        specular,
        specularity,
    )
    return result.reshape(width_x, width_y, block)


def solution(mesh):
    sizes = (mesh.shape["space"], mesh.shape["mrow"], mesh.shape["mcol"])
    in_specs = (
        P("space", None, ("mcol", "mrow")),
        P(None, ("mcol", "mrow")),
        P("mrow", ("mcol", "space")),
        P("space"),
        P("space"),
        P(),
        P(),
    )
    out_specs = P("space", None, ("mrow", "mcol"))
    return jax.shard_map(
        functools.partial(on_device, sizes),
        mesh=mesh,
        in_specs=in_specs,
        out_specs=out_specs,
        check_vma=False,
    )
```

time: 449 us -> 114 us (0.25)
  waiting for transfers between devices: 357 us -> 0 us
  Pallas kernels: 0 us -> 109 us
  local copies, waits for them, and re-layouts: 32.1 us -> 5.15 us
  other arithmetic: 20 us -> 0 us
  matrix products: 19.3 us -> 0 us
  between operations: 13.3 us -> 0.01 us
  starting transfers between devices: 7.05 us -> 0 us
    all_gather x3 -> x0, waiting for transfers between devices: 236 us -> none  [the longest x1 118 us: on_device(): lax.all_gather(collide, 'space', axis=1, tiled=True)]
    reduce_scatter x1 -> x0, waiting for transfers between devices: 117 us -> none  [on_device(): lax.psum_scatter(partial_sums, 'mcol', scatter_dimension=1, tiled=True)]
    pallas_call x0 -> x1, Pallas kernels: none -> 109 us  [on_device(): pl.pallas_call(functools.partial(body, sizes), out_shape=jax.ShapeDtypeSt...]
    dot_general x2 -> x0, matrix products: 19.3 us -> none  [the longest x1 19 us: on_device(): lax.dot_general(column_flat, lax.all_gather(collide, 'space', axis=1, til...]
    gather x2 -> x0, local copies, waits for them, and re-layouts: 13.4 us -> none  [the longest x1 10.8 us: mirror_values(): picked = flipped[wall_tables].astype(jnp.float32)]
    convert_element_type x5 -> x0, other arithmetic: 11.2 us -> none  [the longest x1 6.19 us: upwind(): return result.astype(jnp.bfloat16)]
    transpose x1 -> x0, local copies, waits for them, and re-layouts: 8.66 us -> none  [mirror_values(): flipped = source_rows.T]
    ppermute x2 -> x0, starting transfers between devices: 6.75 us -> none  [the longest x1 5.46 us: extended(): before = lax.ppermute(last, axis, up)]
  transfers between devices with their start and end apart: 6 -> 0, of which waited for: 5 -> 0; matrix products, arithmetic and copies ran while one was open for 7% -> 0% of each run, Pallas kernels for 0% -> 0%
where the time goes in v1:
time: 114 us
  Pallas kernels  109 us (96%)
  local copies, waits for them, and re-layouts  5.15 us (5%)
    pallas_call x1, Pallas kernels, on_device(): pl.pallas_call(functools.partial(body, sizes), out_shape=jax.ShapeDtypeSt...  109 us
    unnamed x1, local copies, waits for them, and re-layouts  2.66 us

profile of v1, /device:TPU:1, one launch (start us, length us, event | category | flops | bytes accessed | tf_op | source)
XLA Modules:
  0.0 113.7 jit_solution(1888330267499231020)
XLA Ops:
  0.0 1.2 %reshape.9.cells_ref = s32[1,384]{1,0:T(1,128)} reshape(s32[384]{0:T(512)} %param.10) | data formatting | bytes 3072 | tf_op jit(solution)/shard_map/reshape | solution.py:467
  1.2 1.3 %reshape.10.wall_ref = s32[1,384]{1,0:T(1,128)} reshape(s32[384]{0:T(512)} %param.11) | data formatting | bytes 3072 | tf_op jit(solution)/shard_map/reshape | solution.py:468
  2.5 108.6 %iterate.1 = bf16[1536,512]{1,0:T(8,128)(2,1)} custom-call(bf16[32,48,512]{2,1,0:T(8,128)(2,1)} %dev_ref.1, f32[2,512]{1,0:T(2,128)} %cour_ref.1, bf16[2048,128]{1,0:T(8,128)(2,1)} %coll_ref.1, s32[1,384]{1,0:T(1,128)} %reshape.9.cells_ref, s32[1,384]{1,0:T(1,128)} %reshape.10.wall_ref, s32[4,8192]{1,0:T(4,128)} %spec_ref.1, f32[4]{0:T(128)} %share_ref.1), custom_call_target="tpu_custom_call" | custom-call | tf_op jit(solution)/shard_map/iterate/pallas_call | solution.py:427
  111.1 2.7 %copy.9 = bf16[32,48,512]{2,1,0:T(8,128)(2,1)} copy(bf16[32,48,512]{2,1,0:T(8,128)(2,1)} %bitcast.1) | data formatting | bytes 3145728

commit v2 on v1

--- a/solution.py
+++ b/solution.py
@@ -10,7 +10,8 @@
 MESH = pl.DeviceIdType.MESH
 F32 = jnp.float32
 BF16 = jnp.bfloat16
-CHUNKS = 4
+PARTS = ((0, 384), (384, 384), (768, 256), (1024, 320), (1344, 192))
+CHUNKS = len(PARTS)
 
 
 def column_of(row, slots):
@@ -23,16 +24,19 @@
 
 def body(
     sizes,
-    dev_ref,
+    dev_hbm,
     cour_ref,
-    coll_ref,
+    coll_hbm,
     cells_ref,
     wall_ref,
     spec_ref,
     share_ref,
-    out_ref,
+    out_hbm,
+    out_buf,
+    dev_ref,
     cols,
     mats,
+    acc,
     read_buf,
     halo,
     msg_out,
@@ -56,16 +60,17 @@
     chip_send,
     chip_recv,
     own_sem,
+    dev_sem,
+    out_sem,
 ):
     n_space, n_row, n_col = sizes
     depth = n_space // 2
     width_x, width_y, block = dev_ref.shape
     cells = width_x * width_y
-    slots = cells_ref.shape[1]
+    slots = cells_ref.shape[0]
     walls, modes = spec_ref.shape
     groups = n_row * n_col
     sub = block // groups
-    chunk = cells // CHUNKS
     far = depth // 2
     half = block // 2
 
@@ -98,12 +103,18 @@
             if dq or dy:
                 peers.append(((y + dy) % n_row, (q + dq) % n_col))
 
+    own_copy = pltpu.make_async_copy(coll_hbm, mats.at[s], own_sem)
+    own_copy.start()
+    dev_copy = pltpu.make_async_copy(dev_hbm, dev_ref, dev_sem)
+    dev_copy.start()
     barrier = pltpu.get_barrier_semaphore()
     for target in (z_next, z_prev, mate_s, other_s):
         pl.semaphore_signal(barrier, inc=1, device_id=(target, y, q), device_id_type=MESH)
     for ty, tq in peers:
         pl.semaphore_signal(barrier, inc=1, device_id=(s, ty, tq), device_id_type=MESH)
     pl.semaphore_wait(barrier, 4 + len(peers))
+    own_copy.wait()
+    dev_copy.wait()
 
     started = []
 
@@ -125,54 +136,75 @@
         size = block if size is None else size
         return pl.ds(pl.multiple_of(blocks[turn] * block + offset, size), size)
 
-    def z_copy(way, group, hop, piece):
-        turn = group * 2 + piece % 2
+    def cells_of(part):
+        start, count = PARTS[part]
+        return pl.ds(start, count)
+
+    def z_copy(way, turn, own, hop):
         if way == 0:
             source = (z + depth - (hop - 1)) % depth
             target = z_next
         else:
             source = (z + hop - 1) % depth
             target = z_prev
-        slot = source * 2 + (h if piece < 2 else 1 - h)
+        slot = source * 2 + (h if own else 1 - h)
         if hop == far:
             rows = rows_of(turn, way * half, half)
         else:
             rows = rows_of(turn)
-        index = ((way * 2 + group) * far + hop - 1) * 4 + piece
-        dst = mats.at[slot, rows]
-        src = coll_ref.at[rows] if hop == 1 and piece < 2 else dst
-        return remote(src, dst, z_send.at[index], z_recv.at[index], (target, y, q))
-
-    def z_start(group, hop, pieces):
-        for piece in pieces:
-            for way in range(2):
-                go(z_copy(way, group, hop, piece))
-
-    def z_serve(group, hop, pieces):
-        for piece in pieces:
-            for way in range(2):
-                z_copy(way, group, hop, piece).wait_recv()
-                if hop < far:
-                    go(z_copy(way, group, hop + 1, piece))
-
-    def x_copy(turn):
-        rows = rows_of(turn)
-        return remote(
-            coll_ref.at[rows],
-            mats.at[s, rows],
-            x_send.at[turn],
-            x_recv.at[turn],
-            (mate_s, y, q),
-        )
+        index = ((way * 4 + turn) * 2 + own) * far + hop - 1
+        ref = mats.at[slot, rows]
+        return remote(ref, ref, z_send.at[index], z_recv.at[index], (target, y, q))
+
+    def z_start(turn, own):
+        for way in range(2):
+            go(z_copy(way, turn, own, 1))
+
+    def z_serve(turn, own, hop):
+        for way in range(2):
+            z_copy(way, turn, own, hop).wait_recv()
+            if hop < far:
+                go(z_copy(way, turn, own, hop + 1))
+            if own and hop == 1 and turn < 3:
+                go(x_copy(turn, 1 + way))
+
+    def z_take(turn):
+        for way in range(2):
+            z_copy(way, turn, 1, 1).wait_recv()
+            go(x_copy(turn, 1 + way))
+
+    def z_pass(turn):
+        for way in range(2):
+            go(z_copy(way, turn, 1, 2))
+
+    def x_copy(turn, kind):
+        source = (z, (z + depth - 1) % depth, (z + 1) % depth)[kind]
+        ref = mats.at[source * 2 + h, rows_of(turn)]
+        index = turn * 3 + kind
+        return remote(ref, ref, x_send.at[index], x_recv.at[index], (mate_s, y, q))
+
+    def x_serve(turn):
+        for way in range(2):
+            x_copy(turn, 1 + way).wait_recv()
+            go(z_copy(way, turn, 0, 2))
+
+    def x_relay(turn):
+        x_copy(turn, 0).wait_recv()
+        for way in range(2):
+            go(z_copy(way, turn, 0, 1))
+
+    def x_finish(turn):
+        x_copy(turn, 0).wait_recv()
 
     def y_copy(way, stage, part):
         target = y_next if way == 0 else y_prev
         if stage == 0:
             owner = y
-            rows = pl.ds(part * chunk, chunk)
+            rows = cells_of(part)
         else:
             owner = y_prev if way == 0 else y_next
-            rows = pl.ds(part * chunk + way * (chunk // 2), chunk // 2)
+            start, count = PARTS[part]
+            rows = pl.ds(start + way * (count // 2), count // 2)
         index = (way * 2 + stage) * CHUNKS + part
         ref = cols.at[owner, rows]
         return remote(ref, ref, y_send.at[index], y_recv.at[index], (s, target, q))
@@ -191,7 +223,7 @@
             y_copy(way, 1, part).wait_recv()
 
     def pair_copy(stage, part):
-        rows = pl.ds(part * chunk, chunk)
+        rows = cells_of(part)
         index = stage * CHUNKS + part
         return remote(
             pair_out.at[stage, rows],
@@ -202,7 +234,7 @@
         )
 
     def chip_copy(part):
-        rows = pl.ds(part * chunk, chunk)
+        rows = cells_of(part)
         return remote(
             chip_out.at[rows],
             chip_in.at[rows],
@@ -212,7 +244,7 @@
         )
 
     def product(turn, part):
-        rows = pl.ds(part * chunk, chunk)
+        rows = cells_of(part)
         total = None
         per = block // mats.shape[2]
         for owner in range(n_row):
@@ -234,12 +266,7 @@
     halo_down = remote(dev_ref.at[0], halo.at[1], halo_send.at[1], halo_recv.at[1], (s_prev, y, q))
     go(halo_up)
     go(halo_down)
-    x_copies = [x_copy(turn) for turn in range(4)]
-    go(x_copies[0])
-    go(x_copies[1])
-    z_start(0, 1, (0, 1))
-    own_copy = pltpu.make_async_copy(coll_ref, mats.at[s], own_sem)
-    own_copy.start()
+    z_start(0, 1)
 
     reach_x = jnp.abs(cour_ref[0:1, :])
     reach_y = jnp.abs(cour_ref[1:2, :])
@@ -261,6 +288,7 @@
         rows = pl.ds(pl.multiple_of(x * width_y, width_y), width_y)
         read_buf[rows, :] = stream(layer(x), layer(x - 1), layer(x + 1))
 
+    z_start(1, 1)
     halo_up.wait_recv()
     halo_down.wait_recv()
     low = jnp.where(s == 0, 0.0, halo[0].astype(F32))
@@ -270,11 +298,7 @@
         layer(width_x - 1), layer(width_x - 2), high
     )
 
-    x_copies[0].wait_recv()
-    x_copies[1].wait_recv()
-    z_start(0, 1, (2, 3))
-
-    cells_row = cells_ref[...].astype(F32)
+    cells_row = cells_ref[...].reshape(1, slots).astype(F32)
     cells_col = column_of(cells_row, slots)
     lane = lax.broadcasted_iota(jnp.int32, (slots, 128), 1).astype(F32)
     pick = jnp.concatenate(
@@ -308,18 +332,19 @@
         go(copy)
         msg_copies.append(copy)
     msg_in[mine] = msg_out[mine]
-    go(x_copies[2])
-    go(x_copies[3])
-
-    z_serve(0, 1, (0, 1, 2))
-
-    wall_col = column_of(wall_ref[...].astype(F32), slots)
+    z_start(2, 1)
+    z_serve(0, 1, 1)
+    z_serve(1, 1, 1)
+
+    wall_col = column_of(wall_ref[...].reshape(1, slots).astype(F32), slots)
     table = spec_ref[:, pl.ds(pl.multiple_of(mine * block, block), block)]
     place = (table // block) * sub + table % sub
     share = jnp.zeros((slots, 128), F32)
     for w in range(walls):
         share = jnp.where(wall_col == float(w), share_ref[w], share)
 
+    z_serve(0, 1, 2)
+    z_serve(1, 1, 2)
     for copy in msg_copies:
         copy.wait_recv()
     received = msg_in[...].astype(F32)
@@ -337,76 +362,120 @@
     emitted = (share * mirrored + (1.0 - share) * diffuse).astype(BF16)
     emitted = jnp.concatenate([emitted, jnp.ones((slots, 128), BF16)], axis=1)
 
-    spread = jnp.broadcast_to(cells_row, (chunk, slots))
-    cell_of = lax.broadcasted_iota(jnp.int32, (chunk, slots), 0).astype(F32)
-
     def patch(part):
-        rows = pl.ds(part * chunk, chunk)
-        place_at = jnp.where(spread == cell_of + float(part * chunk), 1.0, 0.0).astype(BF16)
+        start, count = PARTS[part]
+        rows = cells_of(part)
+        spread = jnp.broadcast_to(cells_row, (count, slots))
+        cell_of = lax.broadcasted_iota(jnp.int32, (count, slots), 0).astype(F32)
+        place_at = jnp.where(spread == cell_of + float(start), 1.0, 0.0).astype(BF16)
         placed = jnp.dot(place_at, emitted, preferred_element_type=F32)
         hole = widen(placed[:, block:], block // 128) > 0.5
         cols[y, rows, :] = jnp.where(
             hole, placed[:, :block], read_buf[rows, :].astype(F32)
         ).astype(BF16)
 
+    def pass_on(part):
+        rows = cells_of(part)
+        pair_out[0, rows, :] = product(0, part)
+        go(pair_copy(0, part))
+        acc[rows, :] = product(1, part)
+
+    def pass_chip(part):
+        rows = cells_of(part)
+        pair_copy(0, part).wait_recv()
+        chip_out[rows, :] = (acc[rows, :] + pair_in[0, rows, :]).astype(BF16)
+        go(chip_copy(part))
+
     patch(0)
     y_start(0)
     patch(1)
     y_start(1)
-    patch(2)
-    patch(3)
-
-    z_serve(0, 1, (3,))
-    z_serve(0, 2, (0, 1, 2, 3))
+    for part in range(2, CHUNKS):
+        patch(part)
+
+    x_serve(0)
+    z_serve(0, 1, 3)
+    z_serve(1, 1, 3)
+    x_serve(1)
+    go(x_copy(0, 0))
+    go(x_copy(1, 0))
+    z_take(2)
+    z_serve(0, 0, 2)
     y_forward(0)
+    z_serve(1, 0, 2)
+    go(x_copy(3, 0))
+    go(x_copy(2, 0))
+    z_serve(0, 0, 3)
+    y_forward(1)
     y_start(2)
-    z_serve(0, 3, (0, 1))
-    y_forward(1)
     y_start(3)
-    z_serve(0, 3, (2, 3))
-    x_copies[2].wait_recv()
-    x_copies[3].wait_recv()
-    z_start(1, 1, (0, 1, 2, 3))
-    z_serve(0, 4, (0, 1, 2, 3))
-    own_copy.wait()
-
-    def pass_on(part):
-        rows = pl.ds(part * chunk, chunk)
-        pair_out[0, rows, :] = product(0, part)
-        go(pair_copy(0, part))
-        total = product(1, part)
-        pair_copy(0, part).wait_recv()
-        chip_out[rows, :] = (total + pair_in[0, rows, :]).astype(BF16)
-        go(chip_copy(part))
-
+    z_serve(1, 0, 3)
+    z_pass(2)
+    z_start(3, 1)
+    x_serve(2)
+    x_relay(3)
+    for turn in range(2):
+        z_serve(turn, 1, 4)
+        z_serve(turn, 0, 4)
+        x_finish(turn)
     y_finish(0)
     pass_on(0)
-    y_forward(2)
-    z_serve(1, 1, (0, 1))
+    z_serve(2, 1, 2)
+    pass_chip(0)
     y_finish(1)
     pass_on(1)
-    z_serve(1, 1, (2, 3))
+    z_serve(3, 1, 1)
+    pass_chip(1)
+    z_serve(2, 0, 2)
+    y_forward(2)
+    z_serve(3, 0, 1)
+    z_serve(2, 1, 3)
     y_forward(3)
-    z_serve(1, 2, (0, 1, 2, 3))
+    y_start(4)
+    z_serve(3, 1, 2)
     y_finish(2)
     pass_on(2)
+    z_serve(2, 0, 3)
+    pass_chip(2)
+    z_serve(3, 0, 2)
     y_finish(3)
     pass_on(3)
-    z_serve(1, 3, (0, 1, 2, 3))
-    z_serve(1, 4, (0, 2))
+    pass_chip(3)
+    z_serve(3, 1, 3)
+    y_forward(4)
+    z_serve(2, 1, 4)
+    z_serve(2, 0, 4)
+    x_finish(2)
+
+    def pass_pair(part):
+        pair_out[1, cells_of(part), :] = product(2, part)
+        go(pair_copy(1, part))
+
+    pass_pair(0)
+    pass_pair(1)
+    z_serve(3, 0, 3)
+    y_finish(4)
+    pass_on(4)
+    pass_pair(2)
+    pass_chip(4)
+    for part in range(3, CHUNKS):
+        pass_pair(part)
+    z_serve(3, 1, 4)
+    z_serve(3, 0, 4)
+    out_copies = []
     for part in range(CHUNKS):
-        rows = pl.ds(part * chunk, chunk)
-        pair_out[1, rows, :] = product(2, part)
-        go(pair_copy(1, part))
-    z_serve(1, 4, (1, 3))
-    for part in range(CHUNKS):
-        rows = pl.ds(part * chunk, chunk)
+        rows = cells_of(part)
         total = product(3, part)
         pair_copy(1, part).wait_recv()
         chip_copy(part).wait_recv()
-        out_ref[rows, :] = (
+        out_buf[rows, :] = (
             total + pair_in[1, rows, :] + chip_in[rows, :].astype(F32)
         ).astype(BF16)
+        copy = pltpu.make_async_copy(out_buf.at[rows], out_hbm.at[rows], out_sem.at[part])
+        copy.start()
+        out_copies.append(copy)
+    for copy in out_copies:
+        copy.wait()
     for copy in started:
         copy.wait_send()
 
@@ -420,6 +489,7 @@
     rows, piece = collide.shape
     vmem = pl.BlockSpec(memory_space=pltpu.VMEM)
     smem = pl.BlockSpec(memory_space=pltpu.SMEM)
+    hbm = pl.BlockSpec(memory_space=pl.ANY)
     dma = pltpu.SemaphoreType.DMA
     hops = 2 * 2 * (n_space // 4) * 4
     ways = 2 * 2 * CHUNKS
@@ -427,11 +497,14 @@
     result = pl.pallas_call(
         functools.partial(body, sizes),
         out_shape=jax.ShapeDtypeStruct((cells, block), BF16),
-        in_specs=[vmem] * 6 + [smem],
-        out_specs=vmem,
+        in_specs=[hbm, vmem, hbm, vmem, vmem, vmem, smem],
+        out_specs=hbm,
         scratch_shapes=[
+            pltpu.VMEM((cells, block), BF16),
+            pltpu.VMEM((width_x, width_y, block), BF16),
             pltpu.VMEM((n_row, cells, block), BF16),
             pltpu.VMEM((n_space, rows, piece), BF16),
+            pltpu.VMEM((cells, block), F32),
             pltpu.VMEM((cells, block), BF16),
             pltpu.VMEM((2, width_y, block), BF16),
             pltpu.VMEM((groups, sub + 16, slots), BF16),
@@ -442,8 +515,8 @@
             pltpu.VMEM((cells, block), BF16),
             dma((hops,)),
             dma((hops,)),
-            dma((4,)),
-            dma((4,)),
+            dma((12,)),
+            dma((12,)),
             dma((2,)),
             dma((2,)),
             dma((groups - 1,)),
@@ -455,6 +528,8 @@
             dma((CHUNKS,)),
             dma((CHUNKS,)),
             dma(()),
+            dma(()),
+            dma((CHUNKS,)),
         ],
         compiler_params=pltpu.CompilerParams(
             collective_id=0, has_side_effects=True, vmem_limit_bytes=60 * 2**20
@@ -464,8 +539,8 @@
         deviation,
         courant,
         collide,
-        hole_cells.reshape(1, slots),
-        hole_wall.reshape(1, slots),
+        hole_cells,
+        hole_wall,
         specular,
         specularity,
     )

time: 114 us -> 100 us (0.88)
  Pallas kernels: 109 us -> 97.5 us
  local copies, waits for them, and re-layouts: 5.15 us -> 2.66 us
    pallas_call x1, Pallas kernels: 109 us -> 97.5 us  [on_device(): pl.pallas_call(functools.partial(body, sizes), out_shape=jax.ShapeDtypeSt...]
    reshape x2 -> x0, local copies, waits for them, and re-layouts: 2.5 us -> none  [the longest x1 1.25 us: on_device(): hole_wall.reshape(1, slots)]
where the time goes in v2:
time: 100 us
  Pallas kernels  97.5 us (98%)
  local copies, waits for them, and re-layouts  2.66 us (3%)
    pallas_call x1, Pallas kernels, on_device(): pl.pallas_call(functools.partial(body, sizes), out_shape=jax.ShapeDtypeSt...  97.5 us
    unnamed x1, local copies, waits for them, and re-layouts  2.66 us

profile of v2, /device:TPU:1, one launch (start us, length us, event | category | flops | bytes accessed | tf_op | source)
XLA Modules:
  0.0 100.1 jit_solution(16711784243996191538)
XLA Ops:
  0.0 97.5 %iterate.1 = bf16[1536,512]{1,0:T(8,128)(2,1)} custom-call(bf16[32,48,512]{2,1,0:T(8,128)(2,1)} %dev_hbm.1, f32[2,512]{1,0:T(2,128)} %cour_ref.1, bf16[2048,128]{1,0:T(8,128)(2,1)} %coll_hbm.1, s32[384]{0:T(512)} %cells_ref.1, s32[384]{0:T(512)} %wall_ref.1, s32[4,8192]{1,0:T(4,128)} %spec_ref.1, f32[4]{0:T(128)} %share_ref.1), custom_call_target="tpu_custom_call" | custom-call | tf_op jit(solution)/shard_map/iterate/pallas_call | solution.py:497
  97.5 2.7 %copy.9 = bf16[32,48,512]{2,1,0:T(8,128)(2,1)} copy(bf16[32,48,512]{2,1,0:T(8,128)(2,1)} %bitcast.1) | data formatting | bytes 3145728

commit v3 on v2

--- a/solution.py
+++ b/solution.py
@@ -152,46 +152,65 @@
             rows = rows_of(turn, way * half, half)
         else:
             rows = rows_of(turn)
-        index = ((way * 4 + turn) * 2 + own) * far + hop - 1
+        index = (turn * 2 + own) * far + hop - 1
         ref = mats.at[slot, rows]
-        return remote(ref, ref, z_send.at[index], z_recv.at[index], (target, y, q))
+        return remote(ref, ref, z_send.at[turn * 2 + own], z_recv.at[index], (target, y, q))
+
+    def z_both(turn, own, hop):
+        index = (turn * 2 + own) * far + hop - 1
+        ref = mats.at[0, pl.ds(0, block if hop == far else 2 * block)]
+        return remote(ref, ref, z_send.at[turn * 2 + own], z_recv.at[index], (z_next, y, q))
+
+    def z_go(turn, own, hop):
+        first = 1 if own or turn == 3 else 2
+        if hop > first:
+            z_both(turn, own, hop - 1).wait_send()
+        for way in range(2):
+            z_copy(way, turn, own, hop).start()
+        if hop == far:
+            started.append(z_both(turn, own, hop))
 
     def z_start(turn, own):
-        for way in range(2):
-            go(z_copy(way, turn, own, 1))
+        z_go(turn, own, 1)
 
     def z_serve(turn, own, hop):
-        for way in range(2):
-            z_copy(way, turn, own, hop).wait_recv()
-            if hop < far:
-                go(z_copy(way, turn, own, hop + 1))
-            if own and hop == 1 and turn < 3:
-                go(x_copy(turn, 1 + way))
+        z_both(turn, own, hop).wait_recv()
+        if hop < far:
+            z_go(turn, own, hop + 1)
+        if own and hop == 1 and turn < 3:
+            x_go(turn)
 
     def z_take(turn):
-        for way in range(2):
-            z_copy(way, turn, 1, 1).wait_recv()
-            go(x_copy(turn, 1 + way))
+        z_both(turn, 1, 1).wait_recv()
+        x_go(turn)
 
     def z_pass(turn):
-        for way in range(2):
-            go(z_copy(way, turn, 1, 2))
+        z_go(turn, 1, 2)
 
     def x_copy(turn, kind):
         source = (z, (z + depth - 1) % depth, (z + 1) % depth)[kind]
         ref = mats.at[source * 2 + h, rows_of(turn)]
-        index = turn * 3 + kind
+        index = turn * 2 + min(kind, 1)
         return remote(ref, ref, x_send.at[index], x_recv.at[index], (mate_s, y, q))
 
+    def x_both(turn):
+        ref = mats.at[0, pl.ds(0, 2 * block)]
+        return remote(
+            ref, ref, x_send.at[turn * 2 + 1], x_recv.at[turn * 2 + 1], (mate_s, y, q)
+        )
+
+    def x_go(turn):
+        for way in range(2):
+            x_copy(turn, 1 + way).start()
+        started.append(x_both(turn))
+
     def x_serve(turn):
-        for way in range(2):
-            x_copy(turn, 1 + way).wait_recv()
-            go(z_copy(way, turn, 0, 2))
+        x_both(turn).wait_recv()
+        z_go(turn, 0, 2)
 
     def x_relay(turn):
         x_copy(turn, 0).wait_recv()
-        for way in range(2):
-            go(z_copy(way, turn, 0, 1))
+        z_go(turn, 0, 1)
 
     def x_finish(turn):
         x_copy(turn, 0).wait_recv()
@@ -205,22 +224,30 @@
             owner = y_prev if way == 0 else y_next
             start, count = PARTS[part]
             rows = pl.ds(start + way * (count // 2), count // 2)
-        index = (way * 2 + stage) * CHUNKS + part
+        index = stage * CHUNKS + part
         ref = cols.at[owner, rows]
-        return remote(ref, ref, y_send.at[index], y_recv.at[index], (s, target, q))
+        return remote(ref, ref, y_send.at[part], y_recv.at[index], (s, target, q))
+
+    def y_both(stage, part):
+        count = PARTS[part][1]
+        ref = cols.at[0, pl.ds(0, count if stage else 2 * count)]
+        return remote(
+            ref, ref, y_send.at[part], y_recv.at[stage * CHUNKS + part], (s, y_next, q)
+        )
 
     def y_start(part):
         for way in range(2):
-            go(y_copy(way, 0, part))
+            y_copy(way, 0, part).start()
 
     def y_forward(part):
+        y_both(0, part).wait_recv()
+        y_both(0, part).wait_send()
         for way in range(2):
-            y_copy(way, 0, part).wait_recv()
-            go(y_copy(way, 1, part))
+            y_copy(way, 1, part).start()
+        started.append(y_both(1, part))
 
     def y_finish(part):
-        for way in range(2):
-            y_copy(way, 1, part).wait_recv()
+        y_both(1, part).wait_recv()
 
     def pair_copy(stage, part):
         rows = cells_of(part)
@@ -228,7 +255,7 @@
         return remote(
             pair_out.at[stage, rows],
             pair_in.at[stage, rows],
-            pair_send.at[index],
+            pair_send.at[part],
             pair_recv.at[index],
             (s, y, core_q),
         )
@@ -256,6 +283,23 @@
                 right,
                 (((1,), (1,)), ((), ())),
                 preferred_element_type=F32,
+            )
+            total = term if total is None else total + term
+        return total
+
+    def product_of(turn, part, offsets):
+        rows = cells_of(part)
+        lanes = 2 * mats.shape[2]
+        total = None
+        for offset in offsets:
+            piece = (z + offset + depth) % depth
+            owner = piece * lanes // block
+            left = cols[owner, rows, pl.ds(pl.multiple_of(piece * lanes % block, lanes), lanes)]
+            right = jnp.concatenate(
+                [mats[2 * piece, rows_of(turn), :], mats[2 * piece + 1, rows_of(turn), :]], axis=1
+            )
+            term = lax.dot_general(
+                left, right, (((1,), (1,)), ((), ())), preferred_element_type=F32
             )
             total = term if total is None else total + term
         return total
@@ -320,18 +364,19 @@
     for e in range(groups):
         msg_out[e, 0:sub, :] = rim[e * sub : (e + 1) * sub].astype(BF16)
         msg_out[e, sub : sub + 16, :] = stats
-    msg_copies = []
-    for index, (ty, tq) in enumerate(peers):
+    for ty, tq in peers:
         copy = remote(
             msg_out.at[tq * n_row + ty],
             msg_in.at[mine],
-            msg_send.at[index],
-            msg_recv.at[index],
+            msg_send,
+            msg_recv,
             (s, ty, tq),
         )
-        go(copy)
-        msg_copies.append(copy)
+        copy.start()
     msg_in[mine] = msg_out[mine]
+    ref = msg_out.at[pl.ds(0, len(peers))]
+    messages = remote(ref, msg_in.at[pl.ds(0, len(peers))], msg_send, msg_recv, (s, y_next, q))
+    started.append(messages)
     z_start(2, 1)
     z_serve(0, 1, 1)
     z_serve(1, 1, 1)
@@ -343,10 +388,7 @@
     for w in range(walls):
         share = jnp.where(wall_col == float(w), share_ref[w], share)
 
-    z_serve(0, 1, 2)
-    z_serve(1, 1, 2)
-    for copy in msg_copies:
-        copy.wait_recv()
+    messages.wait_recv()
     received = msg_in[...].astype(F32)
     inner = received[:, 0:sub, :].reshape(groups * sub, slots).T
     diffuse = jnp.sum(jnp.sum(received[:, sub : sub + 16, :], axis=0), axis=0, keepdims=True)
@@ -377,7 +419,7 @@
     def pass_on(part):
         rows = cells_of(part)
         pair_out[0, rows, :] = product(0, part)
-        go(pair_copy(0, part))
+        pair_copy(0, part).start()
         acc[rows, :] = product(1, part)
 
     def pass_chip(part):
@@ -388,18 +430,20 @@
 
     patch(0)
     y_start(0)
+    z_serve(0, 1, 2)
     patch(1)
     y_start(1)
     for part in range(2, CHUNKS):
         patch(part)
 
+    z_serve(1, 1, 2)
+    go(x_copy(0, 0))
+    go(x_copy(1, 0))
+    z_take(2)
     x_serve(0)
     z_serve(0, 1, 3)
     z_serve(1, 1, 3)
     x_serve(1)
-    go(x_copy(0, 0))
-    go(x_copy(1, 0))
-    z_take(2)
     z_serve(0, 0, 2)
     y_forward(0)
     z_serve(1, 0, 2)
@@ -428,7 +472,38 @@
     pass_chip(1)
     z_serve(2, 0, 2)
     y_forward(2)
+    near = (0, 1, -1)
+    mid = near + (2, -2)
+    rest = (3, -3, 4)
+
+    def early_pair(part):
+        pair_out[1, cells_of(part), :] = product_of(2, part, mid)
+
+    def pass_pair(part):
+        rows = cells_of(part)
+        if part < 3:
+            pair_out[1, rows, :] += product_of(2, part, rest)
+        else:
+            pair_out[1, rows, :] = product(2, part)
+        pair_copy(0, part).wait_send()
+        pair_copy(1, part).start()
+
+    def early_own(part, offsets):
+        acc[cells_of(part), :] = product_of(3, part, offsets)
+
+    def late_own(part):
+        if part < 2:
+            return acc[cells_of(part), :] + product_of(3, part, (2, -2) + rest)
+        if part == 2:
+            return acc[cells_of(part), :] + product_of(3, part, rest)
+        return product(3, part)
+
+    x_finish(2)
+    early_pair(0)
+    early_pair(1)
     z_serve(3, 0, 1)
+    early_own(0, near)
+    early_own(1, near)
     z_serve(2, 1, 3)
     y_forward(3)
     y_start(4)
@@ -437,45 +512,38 @@
     pass_on(2)
     z_serve(2, 0, 3)
     pass_chip(2)
+    early_pair(2)
     z_serve(3, 0, 2)
     y_finish(3)
     pass_on(3)
+    y_forward(4)
     pass_chip(3)
+    early_own(2, mid)
     z_serve(3, 1, 3)
-    y_forward(4)
+    y_finish(4)
+    pass_on(4)
+    z_serve(3, 0, 3)
     z_serve(2, 1, 4)
     z_serve(2, 0, 4)
-    x_finish(2)
-
-    def pass_pair(part):
-        pair_out[1, cells_of(part), :] = product(2, part)
-        go(pair_copy(1, part))
-
     pass_pair(0)
-    pass_pair(1)
-    z_serve(3, 0, 3)
-    y_finish(4)
-    pass_on(4)
-    pass_pair(2)
     pass_chip(4)
-    for part in range(3, CHUNKS):
+    for part in range(1, CHUNKS):
         pass_pair(part)
     z_serve(3, 1, 4)
     z_serve(3, 0, 4)
-    out_copies = []
     for part in range(CHUNKS):
         rows = cells_of(part)
-        total = product(3, part)
+        total = late_own(part)
         pair_copy(1, part).wait_recv()
         chip_copy(part).wait_recv()
         out_buf[rows, :] = (
             total + pair_in[1, rows, :] + chip_in[rows, :].astype(F32)
         ).astype(BF16)
-        copy = pltpu.make_async_copy(out_buf.at[rows], out_hbm.at[rows], out_sem.at[part])
+        copy = pltpu.make_async_copy(out_buf.at[rows], out_hbm.at[rows], out_sem)
         copy.start()
-        out_copies.append(copy)
-    for copy in out_copies:
-        copy.wait()
+    pltpu.make_async_copy(out_buf, out_hbm, out_sem).wait()
+    for part in range(CHUNKS):
+        pair_copy(1, part).wait_send()
     for copy in started:
         copy.wait_send()
 
@@ -491,8 +559,6 @@
     smem = pl.BlockSpec(memory_space=pltpu.SMEM)
     hbm = pl.BlockSpec(memory_space=pl.ANY)
     dma = pltpu.SemaphoreType.DMA
-    hops = 2 * 2 * (n_space // 4) * 4
-    ways = 2 * 2 * CHUNKS
     sub = block // groups
     result = pl.pallas_call(
         functools.partial(body, sizes),
@@ -513,23 +579,23 @@
             pltpu.VMEM((2, cells, block), F32),
             pltpu.VMEM((cells, block), BF16),
             pltpu.VMEM((cells, block), BF16),
-            dma((hops,)),
-            dma((hops,)),
-            dma((12,)),
-            dma((12,)),
+            dma((8,)),
+            dma((8 * (n_space // 4),)),
+            dma((8,)),
+            dma((8,)),
             dma((2,)),
             dma((2,)),
-            dma((groups - 1,)),
-            dma((groups - 1,)),
-            dma((ways,)),
-            dma((ways,)),
+            dma(()),
+            dma(()),
+            dma((CHUNKS,)),
             dma((2 * CHUNKS,)),
+            dma((CHUNKS,)),
             dma((2 * CHUNKS,)),
             dma((CHUNKS,)),
             dma((CHUNKS,)),
             dma(()),
             dma(()),
-            dma((CHUNKS,)),
+            dma(()),
         ],
         compiler_params=pltpu.CompilerParams(
             collective_id=0, has_side_effects=True, vmem_limit_bytes=60 * 2**20

time: 100 us -> 96.7 us (0.967)
  Pallas kernels: 97.5 us -> 93.9 us
    pallas_call x1, Pallas kernels: 97.5 us -> 93.9 us  [on_device(): pl.pallas_call(functools.partial(body, sizes), out_shape=jax.ShapeDtypeSt...]
where the time goes in v3:
time: 96.7 us; the launch traced here: 96.5 us
  Pallas kernels  93.9 us (97%)
  local copies, waits for them, and re-layouts  2.66 us (3%)
    pallas_call x1, Pallas kernels, on_device(): pl.pallas_call(functools.partial(body, sizes), out_shape=jax.ShapeDtypeSt...  93.9 us
    unnamed x1, local copies, waits for them, and re-layouts  2.66 us

profile of v3, /device:TPU:1, one launch (start us, length us, event | category | flops | bytes accessed | tf_op | source)
XLA Modules:
  0.0 96.5 jit_solution(648201017402243890)
XLA Ops:
  0.0 93.9 %iterate.1 = bf16[1536,512]{1,0:T(8,128)(2,1)} custom-call(bf16[32,48,512]{2,1,0:T(8,128)(2,1)} %dev_hbm.1, f32[2,512]{1,0:T(2,128)} %cour_ref.1, bf16[2048,128]{1,0:T(8,128)(2,1)} %coll_hbm.1, s32[384]{0:T(512)} %cells_ref.1, s32[384]{0:T(512)} %wall_ref.1, s32[4,8192]{1,0:T(4,128)} %spec_ref.1, f32[4]{0:T(128)} %share_ref.1), custom_call_target="tpu_custom_call" | custom-call | tf_op jit(solution)/shard_map/iterate/pallas_call | solution.py:563
  93.9 2.7 %copy.9 = bf16[32,48,512]{2,1,0:T(8,128)(2,1)} copy(bf16[32,48,512]{2,1,0:T(8,128)(2,1)} %bitcast.1) | data formatting | bytes 3145728

commit v4 on v3

--- a/solution.py
+++ b/solution.py
@@ -29,10 +29,11 @@
     coll_hbm,
     cells_ref,
     wall_ref,
-    spec_ref,
+    spec_hbm,
     share_ref,
     out_hbm,
     out_buf,
+    spec_ref,
     dev_ref,
     cols,
     mats,
@@ -61,6 +62,7 @@
     chip_recv,
     own_sem,
     dev_sem,
+    spec_sem,
     out_sem,
 ):
     n_space, n_row, n_col = sizes
@@ -68,7 +70,7 @@
     width_x, width_y, block = dev_ref.shape
     cells = width_x * width_y
     slots = cells_ref.shape[0]
-    walls, modes = spec_ref.shape
+    walls, modes = spec_hbm.shape
     groups = n_row * n_col
     sub = block // groups
     far = depth // 2
@@ -107,6 +109,9 @@
     own_copy.start()
     dev_copy = pltpu.make_async_copy(dev_hbm, dev_ref, dev_sem)
     dev_copy.start()
+    columns = pl.ds(pl.multiple_of(mine * block, block), block)
+    spec_copy = pltpu.make_async_copy(spec_hbm.at[:, columns], spec_ref, spec_sem)
+    spec_copy.start()
     barrier = pltpu.get_barrier_semaphore()
     for target in (z_next, z_prev, mate_s, other_s):
         pl.semaphore_signal(barrier, inc=1, device_id=(target, y, q), device_id_type=MESH)
@@ -115,6 +120,7 @@
     pl.semaphore_wait(barrier, 4 + len(peers))
     own_copy.wait()
     dev_copy.wait()
+    spec_copy.wait()
 
     started = []
 
@@ -382,7 +388,7 @@
     z_serve(1, 1, 1)
 
     wall_col = column_of(wall_ref[...].reshape(1, slots).astype(F32), slots)
-    table = spec_ref[:, pl.ds(pl.multiple_of(mine * block, block), block)]
+    table = spec_ref[...]
     place = (table // block) * sub + table % sub
     share = jnp.zeros((slots, 128), F32)
     for w in range(walls):
@@ -416,11 +422,16 @@
             hole, placed[:, :block], read_buf[rows, :].astype(F32)
         ).astype(BF16)
 
+    def pass_first(part):
+        pair_out[0, cells_of(part), :] = product(0, part)
+        pair_copy(0, part).start()
+
+    def pass_second(part):
+        acc[cells_of(part), :] = product(1, part)
+
     def pass_on(part):
-        rows = cells_of(part)
-        pair_out[0, rows, :] = product(0, part)
-        pair_copy(0, part).start()
-        acc[rows, :] = product(1, part)
+        pass_first(part)
+        pass_second(part)
 
     def pass_chip(part):
         rows = cells_of(part)
@@ -458,14 +469,17 @@
     z_start(3, 1)
     x_serve(2)
     x_relay(3)
-    for turn in range(2):
-        z_serve(turn, 1, 4)
-        z_serve(turn, 0, 4)
-        x_finish(turn)
+    z_serve(0, 1, 4)
+    z_serve(0, 0, 4)
+    x_finish(0)
     y_finish(0)
-    pass_on(0)
+    pass_first(0)
+    z_serve(1, 1, 4)
+    z_serve(1, 0, 4)
+    x_finish(1)
+    pass_second(0)
+    pass_chip(0)
     z_serve(2, 1, 2)
-    pass_chip(0)
     y_finish(1)
     pass_on(1)
     z_serve(3, 1, 1)
@@ -491,10 +505,11 @@
     def early_own(part, offsets):
         acc[cells_of(part), :] = product_of(3, part, offsets)
 
+    def more_own(part):
+        acc[cells_of(part), :] += product_of(3, part, (2, -2))
+
     def late_own(part):
-        if part < 2:
-            return acc[cells_of(part), :] + product_of(3, part, (2, -2) + rest)
-        if part == 2:
+        if part < 4:
             return acc[cells_of(part), :] + product_of(3, part, rest)
         return product(3, part)
 
@@ -519,13 +534,17 @@
     y_forward(4)
     pass_chip(3)
     early_own(2, mid)
+    early_own(3, mid)
+    more_own(0)
+    more_own(1)
     z_serve(3, 1, 3)
-    y_finish(4)
-    pass_on(4)
-    z_serve(3, 0, 3)
     z_serve(2, 1, 4)
     z_serve(2, 0, 4)
     pass_pair(0)
+    y_finish(4)
+    pass_first(4)
+    z_serve(3, 0, 3)
+    pass_second(4)
     pass_chip(4)
     for part in range(1, CHUNKS):
         pass_pair(part)
@@ -563,10 +582,11 @@
     result = pl.pallas_call(
         functools.partial(body, sizes),
         out_shape=jax.ShapeDtypeStruct((cells, block), BF16),
-        in_specs=[hbm, vmem, hbm, vmem, vmem, vmem, smem],
+        in_specs=[hbm, vmem, hbm, vmem, vmem, hbm, smem],
         out_specs=hbm,
         scratch_shapes=[
             pltpu.VMEM((cells, block), BF16),
+            pltpu.VMEM((specular.shape[0], block), jnp.int32),
             pltpu.VMEM((width_x, width_y, block), BF16),
             pltpu.VMEM((n_row, cells, block), BF16),
             pltpu.VMEM((n_space, rows, piece), BF16),
@@ -596,6 +616,7 @@
             dma(()),
             dma(()),
             dma(()),
+            dma(()),
         ],
         compiler_params=pltpu.CompilerParams(
             collective_id=0, has_side_effects=True, vmem_limit_bytes=60 * 2**20

time: 96.7 us -> 96.2 us (level)
  no operation moved by 1% of the time
where the time goes in v4:
time: 96.2 us; the launch traced here: 96.1 us
  Pallas kernels  93.4 us (97%)
  local copies, waits for them, and re-layouts  2.66 us (3%)
    pallas_call x1, Pallas kernels, on_device(): pl.pallas_call(functools.partial(body, sizes), out_shape=jax.ShapeDtypeSt...  93.4 us
    unnamed x1, local copies, waits for them, and re-layouts  2.66 us

profile of v4, /device:TPU:1, one launch (start us, length us, event | category | flops | bytes accessed | tf_op | source)
XLA Modules:
  0.0 96.1 jit_solution(8456357603473048290)
XLA Ops:
  0.0 93.4 %iterate.1 = bf16[1536,512]{1,0:T(8,128)(2,1)} custom-call(bf16[32,48,512]{2,1,0:T(8,128)(2,1)} %dev_hbm.1, f32[2,512]{1,0:T(2,128)} %cour_ref.1, bf16[2048,128]{1,0:T(8,128)(2,1)} %coll_hbm.1, s32[384]{0:T(512)} %cells_ref.1, s32[384]{0:T(512)} %wall_ref.1, s32[4,8192]{1,0:T(4,128)} %spec_hbm.1, f32[4]{0:T(128)} %share_ref.1), custom_call_target="tpu_custom_call" | custom-call | tf_op jit(solution)/shard_map/iterate/pallas_call | solution.py:582
  93.4 2.7 %copy.9 = bf16[32,48,512]{2,1,0:T(8,128)(2,1)} copy(bf16[32,48,512]{2,1,0:T(8,128)(2,1)} %bitcast.1) | data formatting | bytes 3145728

commit v5 on v4

--- a/solution.py
+++ b/solution.py
@@ -532,10 +532,10 @@
     y_finish(3)
     pass_on(3)
     y_forward(4)
+    early_own(2, mid)
+    more_own(0)
     pass_chip(3)
-    early_own(2, mid)
     early_own(3, mid)
-    more_own(0)
     more_own(1)
     z_serve(3, 1, 3)
     z_serve(2, 1, 4)
@@ -545,8 +545,9 @@
     pass_first(4)
     z_serve(3, 0, 3)
     pass_second(4)
+    pass_pair(1)
     pass_chip(4)
-    for part in range(1, CHUNKS):
+    for part in range(2, CHUNKS):
         pass_pair(part)
     z_serve(3, 1, 4)
     z_serve(3, 0, 4)

time: 96.2 us -> 95.6 us (level)
  no operation moved by 1% of the time
where the time goes in v5:
time: 95.6 us; the launch traced here: 95.5 us
  Pallas kernels  92.8 us (97%)
  local copies, waits for them, and re-layouts  2.66 us (3%)
    pallas_call x1, Pallas kernels, on_device(): pl.pallas_call(functools.partial(body, sizes), out_shape=jax.ShapeDtypeSt...  92.8 us
    unnamed x1, local copies, waits for them, and re-layouts  2.66 us

profile of v5, /device:TPU:1, one launch (start us, length us, event | category | flops | bytes accessed | tf_op | source)
XLA Modules:
  0.0 95.5 jit_solution(12205928233756584947)
XLA Ops:
  0.0 92.8 %iterate.1 = bf16[1536,512]{1,0:T(8,128)(2,1)} custom-call(bf16[32,48,512]{2,1,0:T(8,128)(2,1)} %dev_hbm.1, f32[2,512]{1,0:T(2,128)} %cour_ref.1, bf16[2048,128]{1,0:T(8,128)(2,1)} %coll_hbm.1, s32[384]{0:T(512)} %cells_ref.1, s32[384]{0:T(512)} %wall_ref.1, s32[4,8192]{1,0:T(4,128)} %spec_hbm.1, f32[4]{0:T(128)} %share_ref.1), custom_call_target="tpu_custom_call" | custom-call | tf_op jit(solution)/shard_map/iterate/pallas_call | solution.py:583
  92.8 2.7 %copy.9 = bf16[32,48,512]{2,1,0:T(8,128)(2,1)} copy(bf16[32,48,512]{2,1,0:T(8,128)(2,1)} %bitcast.1) | data formatting | bytes 3145728
